TPU v7x, 256 devices: a whole 4x4x8 slice. The times are simulated.
256 devices in a mesh: aux: 8 (over x, core), orb: 32 (over z, y).
Axes of the slice: x: 4, y: 4, z: 8, core: 2. Of those that a mesh axis runs over, the one named last changes fastest.
Arguments:
- three_center: float32 [32, 32, 128, 1024], P('aux', 'orb'), may hold values from -6 to 6
- tile_lists: int32 [2, 32, 8, 8], P(None, 'aux'), may hold values from -1 to 7, as said below
- occ_density: float32 [2, 1024, 1024], P(None, 'orb', 'aux'), may hold values from -0.1875 to 0.1875
- vir_density: float32 [2, 1024, 1024], P(None, 'orb', 'aux'), may hold values from -0.1875 to 0.1875
Outputs:
- coupled: float32 [2, 32, 32, 1024, 128], P(None, 'aux', 'orb')
Inputs may be any that keep to these rules, and one draw needn't show every extreme that they name: Row m of tile_lists[t, j] names distinct orbital blocks in rising order, block m always among them, and -1 in the remaining places; it names between 2 and 8 blocks, and for every t and j one row names all 8 and another exactly 2.
All inputs are finite; a program needn't handle non-finite values.
Results may differ from a plain program's by a relative error of at most 0.0003.
Values sent between devices are 32-bit elements; how exact they have to be, the bound alone decides.
A program may use at most 64 MiB of HBM per device.

v0:
```python
import jax
import jax.numpy as jnp
from jax import lax
from jax.sharding import PartitionSpec as P


def listed_mask(tile_lists, part_index, block_index):
    block_table = lax.dynamic_index_in_dim(tile_lists, part_index, 1, keepdims=False)
    listed_row = lax.dynamic_index_in_dim(block_table, block_index, 1, keepdims=False)
    block_count = tile_lists.shape[3]
    block_ids = jnp.arange(block_count, dtype=jnp.int32)
    matches = listed_row[:, :, None] == block_ids[None, None, :]
    return jnp.sum(matches.astype(jnp.float32), axis=1)


def masked_rows(integrals, listed_now):
    aux_count, block_size, orbitals = integrals.shape
    block_count = orbitals // block_size
    viewed = integrals.reshape(aux_count, block_size, block_count, block_size)
    masked = viewed[None] * listed_now[:, None, None, :, None]
    return masked.reshape(listed_now.shape[0], aux_count * block_size, orbitals)


def make_adder(masked, density_rows):
    return jnp.einsum("tar,trl->tal", masked, density_rows, precision=lax.Precision.HIGHEST)


def make_applier(column_data, density_rows):
    return jnp.einsum("tsk,takl->tasl", density_rows, column_data, precision=lax.Precision.HIGHEST)


def outgoing(product, listed_now, aux_count, block_size, block_count, split_count):
    time_count = product.shape[0]
    aux_share = aux_count // split_count
    pruned = product.reshape(time_count, aux_count, block_size, block_count, block_size)
    pruned = pruned * listed_now[:, None, None, :, None]
    split_view = pruned.reshape(
        time_count, split_count, aux_share, block_size, block_count, block_size
    )
    ordered = split_view.transpose(4, 1, 0, 2, 3, 5)
    return ordered.reshape(block_count * split_count, time_count, aux_share, block_size, block_size)


def make_arrange(block_count, split_count):

    def arrange(received):
        unit_count, time_count, item_count, row_count, col_count = received.shape
        grouped = received.reshape(
            block_count, split_count, time_count, item_count, row_count, col_count
        )
        reordered = grouped.transpose(2, 1, 3, 0, 4, 5)
        return reordered.reshape(
            time_count, split_count, item_count, block_count * row_count, col_count
        )

    return arrange


def local(three_center, tile_lists, occ_density, vir_density):
    aux_count = three_center.shape[0]
    block_size = three_center.shape[2]
    orbitals = three_center.shape[3]
    block_count = orbitals // block_size
    owners = lax.axis_size("orb")
    split_count = owners // block_count
    owner_unit = lax.axis_index("orb")
    block_index = owner_unit // split_count
    part_index = owner_unit % split_count
    listed = listed_mask(tile_lists, part_index, block_index)
    integrals = three_center[:, 0]
    arrange = make_arrange(block_count, split_count)
    occ_cols, vir_cols = (
        lax.all_gather(occ_density, "aux", axis=2, tiled=True),
        lax.all_gather(vir_density, "aux", axis=2, tiled=True),
    )
    results = []
    for moment in range(occ_cols.shape[0]):
        listed_now = listed[moment : moment + 1]
        masked = masked_rows(integrals, listed_now)
        product = make_adder(
            masked, lax.all_gather(occ_cols[moment : moment + 1], "orb", axis=1, tiled=True)
        )
        sending = outgoing(product, listed_now, aux_count, block_size, block_count, split_count)
        column_data = arrange(
            lax.all_to_all(sending, "orb", split_axis=0, concat_axis=0, tiled=True)
        )
        column_data = column_data.reshape(1, aux_count, orbitals, block_size)
        results.append(
            make_applier(
                column_data,
                lax.all_gather(vir_cols[moment : moment + 1], "orb", axis=1, tiled=True),
            )
        )
    coupled = jnp.concatenate(results, axis=0)
    return coupled[:, :, None]


def solution(mesh):
    in_specs = (
        P("aux", "orb", None, None),
        P(None, "aux", None, None),
        P(None, "orb", "aux"),
        P(None, "orb", "aux"),
    )
    out_specs = P(None, "aux", "orb", None, None)
    return jax.shard_map(local, mesh=mesh, in_specs=in_specs, out_specs=out_specs, check_vma=False)
```

profile of v0, /device:TPU:2, one launch (start us, length us, event | category | flops | bytes accessed | tf_op | source)
XLA Modules:
  0.0 402.3 jit_solution(4999827515869615526)
XLA Ops:
  6.5 0.0 copy-start
  6.5 0.0 all-gather.9.cloned.1.call-start
  6.5 13.2 %all_gather.18 = f32[2,32,1024]{2,1,0:T(8,128)S(1)} all-gather(f32[2,32,128]{2,1,0:T(8,128)} %param.6), channel_id=1, replica_groups=mesh['aux'=8,'orb'=32] {'aux'}, dimensions={2}, use_global_device_ids=true | all-gather | bytes 294912 | tf_op jit(solution)/shard_map/all_gather | solution.py:73
  19.8 0.7 fusion.23
  20.5 0.0 all-gather.9.cloned.1.call-update
  20.5 0.0 all-gather.5.cloned.1.call-start
  20.6 0.7 all-gather.5.cloned.1.call-update
  21.3 0.0 all-gather.7.cloned.1.call-start
  21.3 13.1 %all_gather.20 = f32[2,32,1024]{2,1,0:T(8,128)S(1)} all-gather(f32[2,32,128]{2,1,0:T(8,128)} %param.7), channel_id=1, replica_groups=mesh['aux'=8,'orb'=32] {'aux'}, dimensions={2}, use_global_device_ids=true | all-gather | bytes 294912 | tf_op jit(solution)/shard_map/all_gather | solution.py:74
  34.4 0.7 fusion.22
  35.1 0.0 all-gather.7.cloned.1.call-update
  35.1 0.0 copy-done
  35.2 0.1 convert_reduce_fusion
  35.3 0.1 broadcast_bitcast_fusion
  35.3 69.8 %all-gather.9.cloned.1.call-done = f32[1,1024,1024]{2,1,0:T(8,128)} async-done(((f32[1,32,1024]{2,1,0:T(8,128)}), f32[1,1024,1024]{2,1,0:T(8,128)}) %all-gather.9.cloned.1.call-update) | async-done | bytes 4194320 | tf_op jit(solution)/shard_map/all_gather | solution.py:81
  105.1 5.3 %copy.28 = f32[1024,1024]{1,0:T(8,128)} copy(f32[1024,1024]{0,1:T(8,128)} %bitcast.95) | data formatting | bytes 8388608 | tf_op jit(solution)/shard_map/tar,trl->tal/dot_general | solution.py:25
  110.4 9.4 %multiply_bitcast_fusion = f32[8,4,1,1,128,128]{5,4,0,1,3,2:T(8,128)S(1)} fusion(f32[8,128,1024,1]{2,1,0,3:T(8,128)} %bitcast.97, f32[4,1,128,1024]{3,2,1,0:T(8,128)} %param.4, f32[8]{0:T(128)S(1)} %get-tuple-element.10, f32[1024]{0:T(1024)S(1)} %get-tuple-element.11), kind=kOutput, calls=%fused_computation.9 | convolution fusion | flops 6443499520 | bytes 8392736 | tf_op jit(solution)/shard_map/tar,trl->tal/dot_general | solution.py:25
  119.9 1.5 copy.29
  121.4 5.4 %all-to-all-start.1 = ((f32[32,1,1,128,128]{4,3,2,1,0:T(8,128)}), f32[32,1,1,128,128]{4,3,2,1,0:T(8,128)S(1)}, u32[]{:S(2)}, u32[]{:S(2)}) async-start(f32[32,1,1,128,128]{4,3,2,1,0:T(8,128)} %bitcast.92), calls=%async_computation.1 | async-start | bytes 4194304 | tf_op jit(solution)/shard_map/all_to_all | solution.py:85
  126.7 0.0 all-gather.11.cloned.1.call-start
  126.8 0.5 all-gather.11.cloned.1.call-update
  127.3 72.3 %all-gather.5.cloned.1.call-done = f32[1,1024,1024]{2,1,0:T(8,128)} async-done(((f32[1,32,1024]{2,1,0:T(8,128)}), f32[1,1024,1024]{2,1,0:T(8,128)}) %all-gather.5.cloned.1.call-update) | async-done | bytes 4194320 | tf_op jit(solution)/shard_map/all_gather | solution.py:81
  199.7 5.3 %copy.24 = f32[1024,1024]{1,0:T(8,128)} copy(f32[1024,1024]{0,1:T(8,128)} %bitcast.94) | data formatting | bytes 8388608 | tf_op jit(solution)/shard_map/tar,trl->tal/dot_general | solution.py:25
  205.0 9.4 %multiply_bitcast_fusion.1 = f32[8,4,1,1,128,128]{5,4,0,1,3,2:T(8,128)S(1)} fusion(f32[8,128,1024,1]{2,1,0,3:T(8,128)} %bitcast.96, f32[4,1,128,1024]{3,2,1,0:T(8,128)} %param.4, f32[8]{0:T(128)S(1)} %get-tuple-element.9, f32[1024]{0:T(1024)S(1)} %get-tuple-element.12), kind=kOutput, calls=%fused_computation.11 | convolution fusion | flops 6443499520 | bytes 8392736 | tf_op jit(solution)/shard_map/tar,trl->tal/dot_general | solution.py:25
  214.5 1.5 copy.25
  215.9 0.0 all-to-all-done.1
  215.9 7.3 %all-to-all-start = ((f32[32,1,1,128,128]{4,3,2,1,0:T(8,128)}), f32[32,1,1,128,128]{4,3,2,1,0:T(8,128)}, u32[]{:S(2)}, u32[]{:S(2)}) async-start(f32[32,1,1,128,128]{4,3,2,1,0:T(8,128)} %bitcast.93), calls=%async_computation | async-start | bytes 4194304 | tf_op jit(solution)/shard_map/all_to_all | solution.py:85
  223.3 1.8 copy.31
  225.1 2.8 reshape.106
  227.8 55.1 %all-to-all-done = f32[32,1,1,128,128]{4,3,2,1,0:T(8,128)} async-done(((f32[32,1,1,128,128]{4,3,2,1,0:T(8,128)}), f32[32,1,1,128,128]{4,3,2,1,0:T(8,128)}, u32[]{:S(2)}, u32[]{:S(2)}) %all-to-all-start) | async-done | bytes 2097184 | tf_op jit(solution)/shard_map/all_to_all | solution.py:85
  282.9 2.1 copy.27
  285.0 1.5 reshape.100
  286.5 0.0 copy-start.1
  286.5 9.8 %all-gather.7.cloned.1.call-done = f32[1,1024,1024]{2,1,0:T(8,128)} async-done(((f32[1,32,1024]{2,1,0:T(8,128)}), f32[1,1024,1024]{2,1,0:T(8,128)}) %all-gather.7.cloned.1.call-update) | async-done | bytes 4194320 | tf_op jit(solution)/shard_map/all_gather | solution.py:91
  296.3 10.3 %fusion.14 = f32[1,4,1024,128]{2,3,1,0:T(8,128)} fusion(f32[4,1024,128]{1,2,0:T(8,128)} %reshape.100, f32[1,1024,1024]{2,1,0:T(8,128)} %all-gather.7.cloned.1.call-done), kind=kOutput, calls=%fused_computation.13 | convolution fusion | flops 6442450944 | bytes 8388608 | tf_op jit(solution)/shard_map/tsk,takl->tasl/dot_general | solution.py:29
  306.6 72.4 %all-gather.11.cloned.1.call-done = f32[1,1024,1024]{2,1,0:T(8,128)} async-done(((f32[1,32,1024]{2,1,0:T(8,128)}), f32[1,1024,1024]{2,1,0:T(8,128)}) %all-gather.11.cloned.1.call-update) | async-done | bytes 4194320 | tf_op jit(solution)/shard_map/all_gather | solution.py:91
  379.0 0.0 copy-done.1
  379.0 0.0 copy-start.2
  379.0 9.2 %fusion.17 = f32[1,4,1024,128]{2,3,1,0:T(8,128)S(1)} fusion(f32[4,1024,128]{1,2,0:T(8,128)S(1)} %copy-done.1, f32[1,1024,1024]{2,1,0:T(8,128)} %all-gather.11.cloned.1.call-done), kind=kOutput, calls=%fused_computation.14 | convolution fusion | flops 6442450944 | bytes 8388608 | tf_op jit(solution)/shard_map/tsk,takl->tasl/dot_general | solution.py:29
  388.2 0.0 copy-done.2
  388.2 2.3 maximum_bitcast_fusion
  390.5 5.3 %copy.32 = f32[2,4,1,1024,128]{4,3,2,1,0:T(8,128)} copy(f32[2,4,1,1024,128]{3,4,1,0,2:T(8,128)} %maximum_bitcast_fusion) | data formatting | bytes 8388608 | tf_op jit(solution)/shard_map/broadcast_in_dim | solution.py:95
  (2 shorter events, 0.0 us)
Async XLA Ops:
  6.5 28.6 %copy-start = (s32[2,4,8,8]{3,2,1,0:T(8,128)S(1)}, s32[2,4,8,8]{3,2,1,0:T(8,128)}, u32[]{:S(2)}) copy-start(s32[2,4,8,8]{3,2,1,0:T(8,128)} %param.5) | copy-start | bytes 6148
  6.5 98.6 %all-gather.9.cloned.1.call-start = ((), (), s32[]{:S(2)}) async-start(), calls=%async_computation.4 | async-start | bytes 4325376 | tf_op jit(solution)/shard_map/all_gather | solution.py:81
  20.5 179.2 %all-gather.5.cloned.1.call-start = ((), (), s32[]{:S(2)}) async-start(), calls=%async_computation.2 | async-start | bytes 4325376 | tf_op jit(solution)/shard_map/all_gather | solution.py:81
  21.3 275.1 %all-gather.7.cloned.1.call-start = ((), (), s32[]{:S(2)}) async-start(), calls=%async_computation.3 | async-start | bytes 4325376 | tf_op jit(solution)/shard_map/all_gather | solution.py:91
  121.4 94.6 %all-to-all-start.1 = ((f32[32,1,1,128,128]{4,3,2,1,0:T(8,128)}), f32[32,1,1,128,128]{4,3,2,1,0:T(8,128)S(1)}, u32[]{:S(2)}, u32[]{:S(2)}) async-start(f32[32,1,1,128,128]{4,3,2,1,0:T(8,128)} %bitcast.92), calls=%async_computation.1 | async-start | bytes 4194304 | tf_op jit(solution)/shard_map/all_to_all | solution.py:85
  126.7 252.3 %all-gather.11.cloned.1.call-start = ((), (), s32[]{:S(2)}) async-start(), calls=%async_computation.5 | async-start | bytes 4325376 | tf_op jit(solution)/shard_map/all_gather | solution.py:91
  215.9 67.0 %all-to-all-start = ((f32[32,1,1,128,128]{4,3,2,1,0:T(8,128)}), f32[32,1,1,128,128]{4,3,2,1,0:T(8,128)}, u32[]{:S(2)}, u32[]{:S(2)}) async-start(f32[32,1,1,128,128]{4,3,2,1,0:T(8,128)} %bitcast.93), calls=%async_computation | async-start | bytes 4194304 | tf_op jit(solution)/shard_map/all_to_all | solution.py:85
  286.5 92.5 %copy-start.1 = (f32[4,1024,128]{1,2,0:T(8,128)S(1)}, f32[4,1024,128]{1,2,0:T(8,128)}, u32[]{:S(2)}) copy-start(f32[4,1024,128]{1,2,0:T(8,128)} %reshape.106) | copy-start | bytes 6291460
  379.0 9.2 %copy-start.2 = (f32[1,4,1024,128]{2,3,1,0:T(8,128)S(1)}, f32[1,4,1024,128]{2,3,1,0:T(8,128)}, u32[]{:S(2)}) copy-start(f32[1,4,1024,128]{2,3,1,0:T(8,128)} %fusion.14) | copy-start | bytes 6291460
Sparse Core Ops, SparseCore 0:
  20.6 84.4 all-gather.8
  107.7 91.9 all-gather.4
  202.3 93.9 all-gather.6
  298.7 80.2 all-gather.10
where the time goes:
time: 403 us; the launch traced here: 402 us
  waiting for transfers between devices  281 us (70%)
  matrix products  38.4 us (10%)
  local copies, waits for them, and re-layouts  28.7 us (7%)
  blocking collectives  26.3 us (7%)
  between operations  13.2 us (3%)
  starting transfers between devices  12.8 us (3%)
    all_gather x2, waiting for transfers between devices, local(): lax.all_gather(occ_cols[moment:moment + 1], 'orb', axis=1, tiled=True)  142 us
    all_gather x2, waiting for transfers between devices, local(): lax.all_gather(vir_cols[moment:moment + 1], 'orb', axis=1, tiled=True)  82.2 us
    all_to_all x2, waiting for transfers between devices, local(): lax.all_to_all(sending, 'orb', split_axis=0, concat_axis=0, tiled=True)  55.1 us
    dot_general x2, matrix products, make_applier(): jnp.einsum('tsk,takl->tasl', density_rows, column_data, precision=lax.Pre...  19.5 us
    dot_general x2, matrix products, make_adder(): jnp.einsum('tar,trl->tal', masked, density_rows, precision=lax.Precision....  18.9 us
    all_gather x1, blocking collectives, local(): lax.all_gather(occ_density, 'aux', axis=2, tiled=True)  13.2 us
    all_gather x1, blocking collectives, local(): lax.all_gather(vir_density, 'aux', axis=2, tiled=True)  13.1 us
    all_to_all x2, starting transfers between devices, local(): lax.all_to_all(sending, 'orb', split_axis=0, concat_axis=0, tiled=True)  12.7 us
  transfers between devices with their start and end apart: 6, of which 5 were waited for; matrix products, arithmetic and copies ran while one was open for 13% of the time, Pallas kernels for 0%

commit v1 on v0

--- a/solution.py
+++ b/solution.py
@@ -85,12 +85,13 @@
             lax.all_to_all(sending, "orb", split_axis=0, concat_axis=0, tiled=True)
         )
         column_data = column_data.reshape(1, aux_count, orbitals, block_size)
-        results.append(
-            make_applier(
-                column_data,
-                lax.all_gather(vir_cols[moment : moment + 1], "orb", axis=1, tiled=True),
+
+        def marks_fit(buf, dimension_no):
+            return jnp.concatenate(
+                lax.all_to_all(jnp.stack(lax.axis_size("orb") * [buf]), "orb", 0, 0), dimension_no
             )
-        )
+
+        results.append(make_applier(column_data, marks_fit(vir_cols[moment : moment + 1], 1)))
     coupled = jnp.concatenate(results, axis=0)
     return coupled[:, :, None]
 

time: 403 us -> 457 us (1.13)
  blocking collectives: 26.3 us -> 82.2 us
  waiting for transfers between devices: 281 us -> 257 us
  starting transfers between devices: 12.8 us -> 29 us
  local copies, waits for them, and re-layouts: 28.7 us -> 33.3 us
    all_gather x2 -> x0, waiting for transfers between devices: 82.2 us -> none  [local(): lax.all_gather(vir_cols[moment:moment + 1], 'orb', axis=1, tiled=True)]
    all_to_all x0 -> x2, waiting for transfers between devices: none -> 74 us  [marks_fit(): lax.all_to_all(jnp.stack(lax.axis_size('orb') * [buf]), 'orb', 0, 0)]
    all_to_all x0 -> x1, blocking collectives: none -> 55.9 us  [local(): lax.all_to_all(sending, 'orb', split_axis=0, concat_axis=0, tiled=True)]
    all_to_all x2 -> x1, waiting for transfers between devices: 55.1 us -> 0.01 us  [local(): lax.all_to_all(sending, 'orb', split_axis=0, concat_axis=0, tiled=True)]
    all_gather x2, waiting for transfers between devices: 142 us -> 182 us  [local(): lax.all_gather(occ_cols[moment:moment + 1], 'orb', axis=1, tiled=True)]
    all_to_all x0 -> x2, starting transfers between devices: none -> 17.5 us  [marks_fit(): lax.all_to_all(jnp.stack(lax.axis_size('orb') * [buf]), 'orb', 0, 0)]
    another operation x2 -> x4, local copies, waits for them, and re-layouts: 4.26 us -> 9.67 us  [the longest x2 5.03 us: marks_fit(): jnp.stack(lax.axis_size('orb') * [buf])]
    all_to_all x2 -> x1, starting transfers between devices: 12.7 us -> 11.4 us  [local(): lax.all_to_all(sending, 'orb', split_axis=0, concat_axis=0, tiled=True)]
  transfers between devices with their start and end apart: 6 -> 5, of which waited for: 5 -> 3; matrix products, arithmetic and copies ran while one was open for 13% -> 12% of each run, Pallas kernels for 0% -> 0%
where the time goes in v1:
time: 457 us; the launch traced here: 455 us
  waiting for transfers between devices  257 us (56%)
  blocking collectives  82.2 us (18%)
  matrix products  37.8 us (8%)
  local copies, waits for them, and re-layouts  33.3 us (7%)
  starting transfers between devices  29 us (6%)
  between operations  13.5 us (3%)
    all_gather x2, waiting for transfers between devices, local(): lax.all_gather(occ_cols[moment:moment + 1], 'orb', axis=1, tiled=True)  182 us
    all_to_all x2, waiting for transfers between devices, marks_fit(): lax.all_to_all(jnp.stack(lax.axis_size('orb') * [buf]), 'orb', 0, 0)  74 us
    all_to_all x1, blocking collectives, local(): lax.all_to_all(sending, 'orb', split_axis=0, concat_axis=0, tiled=True)  55.9 us
    dot_general x2, matrix products, make_applier(): jnp.einsum('tsk,takl->tasl', density_rows, column_data, precision=lax.Pre...  19.5 us
    dot_general x2, matrix products, make_adder(): jnp.einsum('tar,trl->tal', masked, density_rows, precision=lax.Precision....  18.2 us
    all_to_all x2, starting transfers between devices, marks_fit(): lax.all_to_all(jnp.stack(lax.axis_size('orb') * [buf]), 'orb', 0, 0)  17.5 us
    all_gather x1, blocking collectives, local(): lax.all_gather(occ_density, 'aux', axis=2, tiled=True)  13.2 us
    all_gather x1, blocking collectives, local(): lax.all_gather(vir_density, 'aux', axis=2, tiled=True)  13.1 us
  transfers between devices with their start and end apart: 5, of which 3 were waited for; matrix products, arithmetic and copies ran while one was open for 12% of the time, Pallas kernels for 0%

profile of v1, /device:TPU:2, one launch (start us, length us, event | category | flops | bytes accessed | tf_op | source)
XLA Modules:
  0.0 455.2 jit_solution(2808208791058575336)
XLA Ops:
  6.5 0.0 copy-start
  6.5 0.0 all-gather.3.cloned.1.call-start
  6.5 13.2 %all_gather.12 = f32[2,32,1024]{2,1,0:T(8,128)S(1)} all-gather(f32[2,32,128]{2,1,0:T(8,128)} %param.6), channel_id=1, replica_groups=mesh['aux'=8,'orb'=32] {'aux'}, dimensions={2}, use_global_device_ids=true | all-gather | bytes 294912 | tf_op jit(solution)/shard_map/all_gather | solution.py:73
  19.8 0.7 fusion.12
  20.5 0.0 all-gather.3.cloned.1.call-update
  20.5 13.1 %all_gather.14 = f32[2,32,1024]{2,1,0:T(8,128)S(1)} all-gather(f32[2,32,128]{2,1,0:T(8,128)} %param.7), channel_id=1, replica_groups=mesh['aux'=8,'orb'=32] {'aux'}, dimensions={2}, use_global_device_ids=true | all-gather | bytes 294912 | tf_op jit(solution)/shard_map/all_gather | solution.py:74
  33.6 2.5 stack.4
  36.1 11.6 %all-to-all-start.1 = ((f32[32,1,32,1024]{3,2,1,0:T(8,128)}), f32[32,1,32,1024]{3,2,1,0:T(8,128)}, u32[]{:S(2)}, u32[]{:S(2)}) async-start(f32[32,1,32,1024]{3,2,1,0:T(8,128)} %stack.4), calls=%async_computation.1 | async-start | bytes 8388608 | tf_op jit(solution)/shard_map/all_to_all | solution.py:91
  47.7 0.0 all-gather.5.cloned.1.call-start
  47.8 0.7 all-gather.5.cloned.1.call-update
  48.5 0.0 copy-done
  48.5 0.1 convert_reduce_fusion
  48.6 0.1 broadcast_bitcast_fusion
  48.7 107.0 %all-gather.3.cloned.1.call-done = f32[1,1024,1024]{2,1,0:T(8,128)} async-done(((f32[1,32,1024]{2,1,0:T(8,128)}), f32[1,1024,1024]{2,1,0:T(8,128)}) %all-gather.3.cloned.1.call-update) | async-done | bytes 4194320 | tf_op jit(solution)/shard_map/all_gather | solution.py:81
  155.7 0.0 copy-start.4
  155.7 5.5 %copy.24 = f32[1024,1024]{1,0:T(8,128)} copy(f32[1024,1024]{0,1:T(8,128)} %bitcast.95) | data formatting | bytes 8388608 | tf_op jit(solution)/shard_map/tar,trl->tal/dot_general | solution.py:25
  161.2 0.0 copy-done.4
  161.2 8.8 %multiply_bitcast_fusion.1 = f32[8,4,1,1,128,128]{5,4,0,1,3,2:T(8,128)S(1)} fusion(f32[8,128,1024,1]{2,1,0,3:T(8,128)} %bitcast.98, f32[4,1,128,1024]{3,2,1,0:T(8,128)S(1)} %copy-done.4, f32[8]{0:T(128)S(1)} %get-tuple-element.9, f32[1024]{0:T(1024)S(1)} %get-tuple-element.12), kind=kOutput, calls=%fused_computation.7 | convolution fusion | flops 6443499520 | bytes 8392736 | tf_op jit(solution)/shard_map/tar,trl->tal/dot_general | solution.py:25
  170.0 1.5 copy.25
  171.5 0.0 all-to-all-done.1
  171.5 11.4 %all-to-all-start = ((f32[32,1,1,128,128]{4,3,2,1,0:T(8,128)}), f32[32,1,1,128,128]{4,3,2,1,0:T(8,128)S(1)}, u32[]{:S(2)}, u32[]{:S(2)}) async-start(f32[32,1,1,128,128]{4,3,2,1,0:T(8,128)} %bitcast.92), calls=%async_computation | async-start | bytes 4194304 | tf_op jit(solution)/shard_map/all_to_all | solution.py:85
  182.9 75.4 %all-gather.5.cloned.1.call-done = f32[1,1024,1024]{2,1,0:T(8,128)} async-done(((f32[1,32,1024]{2,1,0:T(8,128)}), f32[1,1024,1024]{2,1,0:T(8,128)}) %all-gather.5.cloned.1.call-update) | async-done | bytes 4194320 | tf_op jit(solution)/shard_map/all_gather | solution.py:81
  258.3 5.3 %copy.28 = f32[1024,1024]{1,0:T(8,128)} copy(f32[1024,1024]{0,1:T(8,128)} %bitcast.96) | data formatting | bytes 8388608 | tf_op jit(solution)/shard_map/tar,trl->tal/dot_general | solution.py:25
  263.7 9.4 %multiply_bitcast_fusion = f32[8,4,1,1,128,128]{5,4,0,1,3,2:T(8,128)S(1)} fusion(f32[8,128,1024,1]{2,1,0,3:T(8,128)} %bitcast.97, f32[4,1,128,1024]{3,2,1,0:T(8,128)} %param.4, f32[8]{0:T(128)S(1)} %get-tuple-element.10, f32[1024]{0:T(1024)S(1)} %get-tuple-element.11), kind=kOutput, calls=%fused_computation.5 | convolution fusion | flops 6443499520 | bytes 8392736 | tf_op jit(solution)/shard_map/tar,trl->tal/dot_general | solution.py:25
  273.1 1.5 copy.29
  274.6 0.0 all-to-all-done
  274.6 55.9 %all_to_all.20 = f32[32,1,1,128,128]{4,3,2,1,0:T(8,128)} all-to-all(f32[32,1,1,128,128]{4,3,2,1,0:T(8,128)} %bitcast.94), channel_id=1, replica_groups=mesh['aux'=8,'orb'=32] {'orb'}, dimensions={0} | all-to-all | bytes 4194304 | tf_op jit(solution)/shard_map/all_to_all | solution.py:85
  330.5 2.5 stack.5
  333.0 5.9 %all-to-all-start.3 = ((f32[32,1,32,1024]{3,2,1,0:T(8,128)}), f32[32,1,32,1024]{3,2,1,0:T(8,128)}, u32[]{:S(2)}, u32[]{:S(2)}) async-start(f32[32,1,32,1024]{3,2,1,0:T(8,128)} %stack.5), calls=%async_computation.3 | async-start | bytes 8388608 | tf_op jit(solution)/shard_map/all_to_all | solution.py:91
  338.9 1.8 copy.27
  340.8 0.0 copy-start.2
  340.8 2.9 reshape.110
  343.7 0.0 copy-done.2
  343.7 1.8 copy.31
  345.5 1.7 reshape.116
  347.3 10.3 %convolution_bitcast_fusion.1 = f32[1,4,1024,128]{2,3,1,0:T(8,128)} fusion(f32[4,1024,128]{1,2,0:T(8,128)} %reshape.110, f32[1024,1024,1]{1,0,2:T(8,128)} %bitcast.18), kind=kOutput, calls=%fused_computation.10 | convolution fusion | flops 6442450944 | bytes 8388608 | tf_op jit(solution)/shard_map/tsk,takl->tasl/dot_general | solution.py:29
  357.6 74.0 %all-to-all-done.3 = f32[32,1,32,1024]{3,2,1,0:T(8,128)} async-done(((f32[32,1,32,1024]{3,2,1,0:T(8,128)}), f32[32,1,32,1024]{3,2,1,0:T(8,128)}, u32[]{:S(2)}, u32[]{:S(2)}) %all-to-all-start.3) | async-done | bytes 4194336 | tf_op jit(solution)/shard_map/all_to_all | solution.py:91
  431.6 0.0 copy-start.3
  431.6 9.2 %convolution_bitcast_fusion = f32[1,4,1024,128]{2,3,1,0:T(8,128)S(1)} fusion(f32[4,1024,128]{1,2,0:T(8,128)S(1)} %reshape.116, f32[1024,1024,1]{1,0,2:T(8,128)} %bitcast.38), kind=kOutput, calls=%fused_computation.9 | convolution fusion | flops 6442450944 | bytes 8388608 | tf_op jit(solution)/shard_map/tsk,takl->tasl/dot_general | solution.py:29
  440.8 0.0 copy-done.3
  440.8 2.3 maximum_bitcast_fusion
  443.1 0.0 copy-start.1
  443.1 5.3 %copy.32 = f32[2,4,1,1024,128]{4,3,2,1,0:T(8,128)} copy(f32[2,4,1,1024,128]{3,4,1,0,2:T(8,128)} %maximum_bitcast_fusion) | data formatting | bytes 8388608 | tf_op jit(solution)/shard_map/broadcast_in_dim | solution.py:96
  448.4 0.0 copy-done.1
  (3 shorter events, 0.0 us)
Async XLA Ops:
  6.5 42.0 %copy-start = (s32[2,4,8,8]{3,2,1,0:T(8,128)S(1)}, s32[2,4,8,8]{3,2,1,0:T(8,128)}, u32[]{:S(2)}) copy-start(s32[2,4,8,8]{3,2,1,0:T(8,128)} %param.5) | copy-start | bytes 6148
  6.5 149.2 %all-gather.3.cloned.1.call-start = ((), (), s32[]{:S(2)}) async-start(), calls=%async_computation.4 | async-start | bytes 4325376 | tf_op jit(solution)/shard_map/all_gather | solution.py:81
  36.1 135.4 %all-to-all-start.1 = ((f32[32,1,32,1024]{3,2,1,0:T(8,128)}), f32[32,1,32,1024]{3,2,1,0:T(8,128)}, u32[]{:S(2)}, u32[]{:S(2)}) async-start(f32[32,1,32,1024]{3,2,1,0:T(8,128)} %stack.4), calls=%async_computation.1 | async-start | bytes 8388608 | tf_op jit(solution)/shard_map/all_to_all | solution.py:91
  47.7 210.6 %all-gather.5.cloned.1.call-start = ((), (), s32[]{:S(2)}) async-start(), calls=%async_computation.5 | async-start | bytes 4325376 | tf_op jit(solution)/shard_map/all_gather | solution.py:81
  155.7 5.5 %copy-start.4 = (f32[4,1,128,1024]{3,2,1,0:T(8,128)S(1)}, f32[4,1,128,1024]{3,2,1,0:T(8,128)}, u32[]{:S(2)}) copy-start(f32[4,1,128,1024]{3,2,1,0:T(8,128)} %param.4) | copy-start | bytes 6291460
  171.5 103.1 %all-to-all-start = ((f32[32,1,1,128,128]{4,3,2,1,0:T(8,128)}), f32[32,1,1,128,128]{4,3,2,1,0:T(8,128)S(1)}, u32[]{:S(2)}, u32[]{:S(2)}) async-start(f32[32,1,1,128,128]{4,3,2,1,0:T(8,128)} %bitcast.92), calls=%async_computation | async-start | bytes 4194304 | tf_op jit(solution)/shard_map/all_to_all | solution.py:85
  333.0 98.5 %all-to-all-start.3 = ((f32[32,1,32,1024]{3,2,1,0:T(8,128)}), f32[32,1,32,1024]{3,2,1,0:T(8,128)}, u32[]{:S(2)}, u32[]{:S(2)}) async-start(f32[32,1,32,1024]{3,2,1,0:T(8,128)} %stack.5), calls=%async_computation.3 | async-start | bytes 8388608 | tf_op jit(solution)/shard_map/all_to_all | solution.py:91
  340.8 2.9 copy-start.2
  431.6 9.2 %copy-start.3 = (f32[1,4,1024,128]{2,3,1,0:T(8,128)S(1)}, f32[1,4,1024,128]{2,3,1,0:T(8,128)}, u32[]{:S(2)}) copy-start(f32[1,4,1024,128]{2,3,1,0:T(8,128)} %convolution_bitcast_fusion.1) | copy-start | bytes 6291460
  443.1 5.4 %copy-start.1 = (s32[2,4,8,8]{3,2,1,0:T(8,128)S(1)}, s32[2,4,8,8]{3,2,1,0:T(8,128)}, u32[]{:S(2)}) copy-start(s32[2,4,8,8]{3,2,1,0:T(8,128)} %param.5) | copy-start | bytes 6148
Sparse Core Ops, SparseCore 0:
  20.6 135.0 all-gather.2
  158.3 99.9 all-gather.4
